TPU v7x, 32 devices: a whole 2x2x4 slice. The times are simulated.
32 devices in a mesh: dp: 8 (over z, y), mp: 4 (over x, core).
Axes of the slice: x: 2, y: 2, z: 4, core: 2. Of those that a mesh axis runs over, the one named last changes fastest.
Arguments:
- tokens: bfloat16 [4096, 2048], P('dp'), may hold values from -6 to 6
- text: bfloat16 [2048, 4096], P('dp', 'mp'), may hold values from -6 to 6
- image_seg: int32 [8, 512], P('dp'), may hold values from 0 to 1, never falling along the last dimension, each value on 1 to 320 neighbouring positions
- text_seg: int32 [8, 256], P('dp'), may hold values from 0 to 1, never falling along the last dimension, each value on 1 to 160 neighbouring positions
- w_qkv: bfloat16 [3, 2048, 2048], P(None, 'dp', 'mp'), may hold values from -0.125 to 0.125
- w_out: bfloat16 [2048, 2048], P('mp', 'dp'), may hold values from -1 to 1
- c_q: bfloat16 [2048, 2048], P('dp', 'mp'), may hold values from -0.125 to 0.125
- c_kv: bfloat16 [2, 4096, 2048], P(None, 'dp', 'mp'), may hold values from -0.09375 to 0.09375
- c_out: bfloat16 [2048, 2048], P('mp', 'dp'), may hold values from -1 to 1
- w_up: bfloat16 [2048, 8192], P('dp', 'mp'), may hold values from -0.125 to 0.125
- w_down: bfloat16 [8192, 2048], P('mp', 'dp'), may hold values from -0.0625 to 0.0625
- norm_gain: float32 [4, 2048], replicated, may hold values from 0.25 to 1.75
- norm_bias: float32 [4, 2048], replicated, may hold values from -4 to 4
- out_bias: float32 [3, 2048], replicated, may hold values from -4 to 4
- up_bias: float32 [8192], P('mp'), may hold values from -4 to 4
- cotangent: bfloat16 [4096, 2048], P('dp'), may hold values from -6 to 6
Outputs:
- output: bfloat16 [4096, 2048], P('dp')
- grad_tokens: float32 [4096, 2048], P('dp')
- grad_text: float32 [2048, 4096], P('dp', 'mp')
- grad_w_qkv: float32 [3, 2048, 2048], P(None, 'dp', 'mp')
- grad_w_out: float32 [2048, 2048], P('mp', 'dp')
- grad_c_q: float32 [2048, 2048], P('dp', 'mp')
- grad_c_kv: float32 [2, 4096, 2048], P(None, 'dp', 'mp')
- grad_c_out: float32 [2048, 2048], P('mp', 'dp')
- grad_w_up: float32 [2048, 8192], P('dp', 'mp')
- grad_w_down: float32 [8192, 2048], P('mp', 'dp')
- grad_norm_gain: float32 [4, 2048], replicated
- grad_norm_bias: float32 [4, 2048], replicated
- grad_out_bias: float32 [3, 2048], replicated
- grad_up_bias: float32 [8192], P('mp')
Inputs may be any that keep to these rules, and one draw needn't show every extreme that they name: In each row image_seg is 0 on the first image and 1 on the second; both images are present, and none has more than 320 tokens. In each row text_seg is 0 on the first caption and 1 on the second; both captions are present, and none has more than 160 tokens.
All inputs are finite; a program needn't handle non-finite values.
Results may differ from a plain program's by a relative error of at most 0.02.
Values may be sent and summed in bfloat16 or wider, within the bound.
No kernel may reach another device: no remote copies, remote signals or barrier semaphores. Data moves between devices by JAX's collectives and lax.ppermute only.
A program may use at most 256 MiB of HBM per device.

v0:
```python
import jax
import jax.numpy as jnp
from jax import lax
from jax.sharding import PartitionSpec as P

HD = 128
eps = 1e-05
masked = -1e30


def normalize(values, gain, shift):
    center = values - jnp.mean(values, axis=-1, keepdims=True)
    spread = jnp.mean(center * center, axis=-1, keepdims=True)
    return center * lax.rsqrt(spread + eps) * gain + shift


def gelu_tanh(values):
    return (
        0.5
        * values
        * (1.0 + jnp.tanh(0.7978845608028654 * (values + 0.044715 * values * values * values)))
    )


def heads_sum(partial_value):
    return lax.psum(partial_value, "mp")


def input_sum(partial_value):
    return lax.psum(partial_value, "mp")


def split_heads(values):
    return values.reshape(values.shape[0], values.shape[1] // HD, HD)


def scores_of(queries, key_rows, allowed):
    raw = jnp.einsum(
        "qhd,khd->hqk",
        split_heads(queries),
        split_heads(key_rows),
        preferred_element_type=jnp.float32,
    ) * HD ** (-0.5)
    return jnp.where(allowed[None], raw, masked)


def attend_forward(queries, key_rows, value_rows, allowed):
    scores = scores_of(queries, key_rows, allowed)
    top = jnp.max(scores, axis=-1, keepdims=True)
    expo = jnp.exp(scores - top)
    total = jnp.sum(expo, axis=-1, keepdims=True)
    probs = (expo / total).astype(jnp.bfloat16)
    mixed = jnp.einsum(
        "hqk,khd->qhd", probs, split_heads(value_rows), preferred_element_type=jnp.float32
    )
    return (
        mixed.reshape(queries.shape[0], queries.shape[1]).astype(jnp.bfloat16),
        top + jnp.log(total),
    )


def attend_backward(queries, key_rows, value_rows, grad_mixed, logsum, allowed):
    scores = scores_of(queries, key_rows, allowed)
    probs = jnp.exp(scores - logsum)
    grad_heads = split_heads(grad_mixed)
    grad_values = jnp.einsum(
        "hqk,qhd->khd", probs.astype(jnp.bfloat16), grad_heads, preferred_element_type=jnp.float32
    )
    grad_probs = jnp.einsum(
        "qhd,khd->hqk", grad_heads, split_heads(value_rows), preferred_element_type=jnp.float32
    )
    grad_scores = (
        probs * (grad_probs - jnp.sum(probs * grad_probs, axis=-1, keepdims=True))
    ).astype(jnp.bfloat16)
    grad_queries = jnp.einsum(
        "hqk,khd->qhd", grad_scores, split_heads(key_rows), preferred_element_type=jnp.float32
    ) * HD ** (-0.5)
    grad_keys = jnp.einsum(
        "hqk,qhd->khd", grad_scores, split_heads(queries), preferred_element_type=jnp.float32
    ) * HD ** (-0.5)
    return (
        grad_queries.reshape(queries.shape),
        grad_keys.reshape(key_rows.shape),
        grad_values.reshape(value_rows.shape),
    )


def on_device(
    tokens,
    text,
    image_seg,
    text_seg,
    w_qkv,
    w_out,
    c_q,
    c_kv,
    c_out,
    w_up,
    w_down,
    norm_gain,
    norm_bias,
    out_bias,
    up_bias,
    cotangent,
):
    row_count = image_seg.shape[0]
    length = image_seg.shape[1]
    text_len = text_seg.shape[1]
    gathered = (
        lax.all_gather(w_qkv, "dp", axis=1, tiled=True),
        lax.all_gather(w_out, "dp", axis=1, tiled=True),
        lax.all_gather(c_q, "dp", axis=0, tiled=True),
        lax.all_gather(c_kv, "dp", axis=1, tiled=True),
        lax.all_gather(c_out, "dp", axis=1, tiled=True),
        lax.all_gather(w_up, "dp", axis=0, tiled=True),
        lax.all_gather(w_down, "dp", axis=1, tiled=True),
    )
    full_qkv, full_out, full_cq, full_ckv, full_cout, full_up, full_down = gathered
    words = lax.all_gather(text, "mp", axis=1, tiled=True)
    same_image = image_seg[:, :, None] == image_seg[:, None, :]
    caption = image_seg[:, :, None] == text_seg[:, None, :]
    residual = tokens.astype(jnp.float32)
    width = full_qkv.shape[2]
    normed_one, pull_one = jax.vjp(normalize, residual, norm_gain[0], norm_bias[0])
    hidden_one = normed_one.astype(jnp.bfloat16)
    projected = jnp.einsum(
        "td,cde->cte", hidden_one, full_qkv, preferred_element_type=jnp.float32
    ).astype(jnp.bfloat16)
    self_inputs = (
        projected[0].reshape(row_count, length, width),
        projected[1].reshape(row_count, length, width),
        projected[2].reshape(row_count, length, width),
    )
    self_mixed, self_logsum = lax.map(
        lambda pieces: attend_forward(*pieces), self_inputs + (same_image,)
    )
    self_flat = self_mixed.reshape(row_count * length, width)
    after_self = (
        residual
        + heads_sum(jnp.dot(self_flat, full_out, preferred_element_type=jnp.float32))
        + out_bias[0]
    )
    normed_two, pull_two = jax.vjp(normalize, after_self, norm_gain[1], norm_bias[1])
    hidden_two = normed_two.astype(jnp.bfloat16)
    cross_query = jnp.dot(hidden_two, full_cq, preferred_element_type=jnp.float32).astype(
        jnp.bfloat16
    )
    text_kv = jnp.einsum("td,cde->cte", words, full_ckv, preferred_element_type=jnp.float32).astype(
        jnp.bfloat16
    )
    cross_inputs = (
        cross_query.reshape(row_count, length, width),
        text_kv[0].reshape(row_count, text_len, width),
        text_kv[1].reshape(row_count, text_len, width),
    )
    cross_mixed, cross_logsum = lax.map(
        lambda pieces: attend_forward(*pieces), cross_inputs + (caption,)
    )
    cross_flat = cross_mixed.reshape(row_count * length, width)
    after_cross = (
        after_self
        + heads_sum(jnp.dot(cross_flat, full_cout, preferred_element_type=jnp.float32))
        + out_bias[1]
    )
    normed_three, pull_three = jax.vjp(normalize, after_cross, norm_gain[2], norm_bias[2])
    hidden_three = normed_three.astype(jnp.bfloat16)
    pre_act = jnp.dot(hidden_three, full_up, preferred_element_type=jnp.float32) + up_bias
    activated, pull_gelu = jax.vjp(gelu_tanh, pre_act)
    act_low = activated.astype(jnp.bfloat16)
    after_mlp = (
        after_cross
        + heads_sum(jnp.dot(act_low, full_down, preferred_element_type=jnp.float32))
        + out_bias[2]
    )
    final, pull_four = jax.vjp(normalize, after_mlp, norm_gain[3], norm_bias[3])
    output = final.astype(jnp.bfloat16)
    grad_mlp, gain_four, shift_four = pull_four(cotangent.astype(jnp.float32))
    grad_mlp_low = grad_mlp.astype(jnp.bfloat16)
    grad_down = jnp.einsum("tf,td->fd", act_low, grad_mlp_low, preferred_element_type=jnp.float32)
    grad_act = jnp.einsum("td,fd->tf", grad_mlp_low, full_down, preferred_element_type=jnp.float32)
    grad_pre = pull_gelu(grad_act)[0].astype(jnp.bfloat16)
    up_bias_grad = jnp.sum(grad_pre.astype(jnp.float32), axis=0)
    grad_up = jnp.einsum("td,tf->df", hidden_three, grad_pre, preferred_element_type=jnp.float32)
    grad_hidden_three = input_sum(
        jnp.einsum("tf,df->td", grad_pre, full_up, preferred_element_type=jnp.float32)
    )
    grad_cross_in, gain_three, shift_three = pull_three(grad_hidden_three)
    grad_after_cross = grad_mlp + grad_cross_in
    grad_cross_low = grad_after_cross.astype(jnp.bfloat16)
    grad_cout = jnp.einsum(
        "te,td->ed", cross_flat, grad_cross_low, preferred_element_type=jnp.float32
    )
    grad_cmix = jnp.einsum(
        "td,ed->te", grad_cross_low, full_cout, preferred_element_type=jnp.float32
    ).astype(jnp.bfloat16)
    cq_grad, ck_grad, cv_grad = lax.map(
        lambda pieces: attend_backward(*pieces),
        cross_inputs + (grad_cmix.reshape(row_count, length, width), cross_logsum, caption),
    )
    cq_low = cq_grad.reshape(row_count * length, width).astype(jnp.bfloat16)
    ckv_low = jnp.stack(
        [ck_grad.reshape(row_count * text_len, width), cv_grad.reshape(row_count * text_len, width)]
    ).astype(jnp.bfloat16)
    grad_cq = jnp.einsum("td,te->de", hidden_two, cq_low, preferred_element_type=jnp.float32)
    grad_ckv = jnp.einsum("td,cte->cde", words, ckv_low, preferred_element_type=jnp.float32)
    text_term = jnp.einsum("cte,cde->td", ckv_low, full_ckv, preferred_element_type=jnp.float32)
    grad_text = lax.psum_scatter(
        text_term.astype(jnp.bfloat16), "mp", scatter_dimension=1, tiled=True
    ).astype(jnp.float32)
    grad_hidden_two = input_sum(
        jnp.einsum("te,de->td", cq_low, full_cq, preferred_element_type=jnp.float32)
    )
    grad_self_in, gain_two, shift_two = pull_two(grad_hidden_two)
    grad_after_self = grad_after_cross + grad_self_in
    grad_self_low = grad_after_self.astype(jnp.bfloat16)
    grad_wout = jnp.einsum(
        "te,td->ed", self_flat, grad_self_low, preferred_element_type=jnp.float32
    )
    grad_smix = jnp.einsum(
        "td,ed->te", grad_self_low, full_out, preferred_element_type=jnp.float32
    ).astype(jnp.bfloat16)
    sq_grad, sk_grad, sv_grad = lax.map(
        lambda pieces: attend_backward(*pieces),
        self_inputs + (grad_smix.reshape(row_count, length, width), self_logsum, same_image),
    )
    qkv_low = jnp.stack(
        [
            sq_grad.reshape(row_count * length, width),
            sk_grad.reshape(row_count * length, width),
            sv_grad.reshape(row_count * length, width),
        ]
    ).astype(jnp.bfloat16)
    grad_qkv = jnp.einsum("td,cte->cde", hidden_one, qkv_low, preferred_element_type=jnp.float32)
    grad_hidden_one = input_sum(
        jnp.einsum("cte,cde->td", qkv_low, full_qkv, preferred_element_type=jnp.float32)
    )
    grad_in_one, gain_one, shift_one = pull_one(grad_hidden_one)
    grad_tokens = grad_after_self + grad_in_one
    gain_terms = jnp.stack([gain_one, gain_two, gain_three, gain_four])
    shift_terms = jnp.stack([shift_one, shift_two, shift_three, shift_four])
    bias_terms = jnp.stack(
        [
            jnp.sum(grad_after_self, axis=0),
            jnp.sum(grad_after_cross, axis=0),
            jnp.sum(grad_mlp, axis=0),
        ]
    )
    gain_total, shift_total, bias_total, up_total = (
        lax.psum(gain_terms.astype(jnp.bfloat16), "dp").astype(jnp.float32),
        lax.psum(shift_terms.astype(jnp.bfloat16), "dp").astype(jnp.float32),
        lax.psum(bias_terms.astype(jnp.bfloat16), "dp").astype(jnp.float32),
        lax.psum(up_bias_grad.astype(jnp.bfloat16), "dp").astype(jnp.float32),
    )
    sum_qkv, sum_wout, sum_cq, sum_ckv, sum_cout, sum_up, sum_down = (
        lax.psum_scatter(
            grad_qkv.astype(jnp.bfloat16), "dp", scatter_dimension=1, tiled=True
        ).astype(jnp.float32),
        lax.psum_scatter(
            grad_wout.astype(jnp.bfloat16), "dp", scatter_dimension=1, tiled=True
        ).astype(jnp.float32),
        lax.psum_scatter(
            grad_cq.astype(jnp.bfloat16), "dp", scatter_dimension=0, tiled=True
        ).astype(jnp.float32),
        lax.psum_scatter(
            grad_ckv.astype(jnp.bfloat16), "dp", scatter_dimension=1, tiled=True
        ).astype(jnp.float32),
        lax.psum_scatter(
            grad_cout.astype(jnp.bfloat16), "dp", scatter_dimension=1, tiled=True
        ).astype(jnp.float32),
        lax.psum_scatter(
            grad_up.astype(jnp.bfloat16), "dp", scatter_dimension=0, tiled=True
        ).astype(jnp.float32),
        lax.psum_scatter(
            grad_down.astype(jnp.bfloat16), "dp", scatter_dimension=1, tiled=True
        ).astype(jnp.float32),
    )
    return (
        output,
        grad_tokens,
        grad_text,
        sum_qkv,
        sum_wout,
        sum_cq,
        sum_ckv,
        sum_cout,
        sum_up,
        sum_down,
        gain_total,
        shift_total,
        bias_total,
        up_total,
    )


def solution(mesh):
    in_specs = (
        P("dp", None),
        P("dp", "mp"),
        P("dp", None),
        P("dp", None),
        P(None, "dp", "mp"),
        P("mp", "dp"),
        P("dp", "mp"),
        P(None, "dp", "mp"),
        P("mp", "dp"),
        P("dp", "mp"),
        P("mp", "dp"),
        P(),
        P(),
        P(),
        P("mp"),
        P("dp", None),
    )
    out_specs = (
        P("dp", None),
        P("dp", None),
        P("dp", "mp"),
        P(None, "dp", "mp"),
        P("mp", "dp"),
        P("dp", "mp"),
        P(None, "dp", "mp"),
        P("mp", "dp"),
        P("dp", "mp"),
        P("mp", "dp"),
        P(),
        P(),
        P(),
        P("mp"),
    )
    return jax.shard_map(
        on_device, mesh=mesh, in_specs=in_specs, out_specs=out_specs, check_vma=False
    )
```

profile of v0, /device:TPU:0, one launch (start us, length us, event | category | flops | bytes accessed | tf_op | source)
XLA Modules:
  0.0 2109.8 jit_solution(6485817762568258638)
XLA Ops:
  13.9 99.0 %all-gather.9.cloned.1.call-done = bf16[3,2048,512]{1,2,0:T(8,128)(2,1)} async-done(((bf16[3,256,512]{1,2,0:T(8,128)(2,1)}), bf16[3,2048,512]{1,2,0:T(8,128)(2,1)}) %all-gather.9.cloned.1.call-update) | async-done | bytes 6291472 | tf_op jit(solution)/shard_map/all_gather | solution.py:110
  112.9 6.5 fusion.35
  124.3 39.2 %all-gather.11.cloned.1.call-done = bf16[512,2048]{1,0:T(8,128)(2,1)} async-done(((bf16[512,256]{1,0:T(8,128)(2,1)}), bf16[512,2048]{1,0:T(8,128)(2,1)}) %all-gather.11.cloned.1.call-update) | async-done | bytes 2097168 | tf_op jit(solution)/shard_map/all_gather | solution.py:111
  163.5 4.9 fusion.88
  172.5 79.7 %all-reduce.8.cloned.1.call-done = f32[512,2048]{1,0:T(8,128)} async-done(((f32[512,2048]{1,0:T(8,128)}), f32[512,2048]{1,0:T(8,128)}) %all-reduce.8.cloned.1.call-update) | async-done | bytes 4194320 | tf_op jit(solution)/shard_map/psum | solution.py:26
  257.8 45.6 %all-gather.17.cloned.1.call-done = bf16[2048,512]{1,0:T(8,128)(2,1)} async-done(((bf16[256,512]{1,0:T(8,128)(2,1)}), bf16[2048,512]{1,0:T(8,128)(2,1)}) %all-gather.17.cloned.1.call-update) | async-done | bytes 2097168 | tf_op jit(solution)/shard_map/all_gather | solution.py:112
  306.4 19.6 all-gather.15.cloned.1.call-done
  326.0 127.4 %all-gather.13.cloned.1.call-done = bf16[2,4096,512]{1,2,0:T(8,128)(2,1)} async-done(((bf16[2,512,512]{1,2,0:T(8,128)(2,1)}), bf16[2,4096,512]{1,2,0:T(8,128)(2,1)}) %all-gather.13.cloned.1.call-update) | async-done | bytes 8388624 | tf_op jit(solution)/shard_map/all_gather | solution.py:113
  453.4 6.3 fusion.46
  461.3 42.8 %all-gather.19.cloned.1.call-done = bf16[512,2048]{1,0:T(8,128)(2,1)} async-done(((bf16[512,256]{1,0:T(8,128)(2,1)}), bf16[512,2048]{1,0:T(8,128)(2,1)}) %all-gather.19.cloned.1.call-update) | async-done | bytes 2097168 | tf_op jit(solution)/shard_map/all_gather | solution.py:114
  504.0 4.8 fusion.89
  510.5 82.3 %all-reduce.10.cloned.1.call-done = f32[512,2048]{1,0:T(8,128)} async-done(((f32[512,2048]{1,0:T(8,128)}), f32[512,2048]{1,0:T(8,128)}) %all-reduce.10.cloned.1.call-update) | async-done | bytes 4194320 | tf_op jit(solution)/shard_map/psum | solution.py:26
  592.7 4.0 fusion.77
  599.3 120.2 %all-gather.21.cloned.1.call-done = bf16[2048,2048]{1,0:T(8,128)(2,1)} async-done(((bf16[256,2048]{1,0:T(8,128)(2,1)}), bf16[2048,2048]{1,0:T(8,128)(2,1)}) %all-gather.21.cloned.1.call-update) | async-done | bytes 8388624 | tf_op jit(solution)/shard_map/all_gather | solution.py:115
  719.5 11.2 fusion.69
  730.7 113.8 %all-gather.23.cloned.1.call-done = bf16[2048,2048]{1,0:T(8,128)(2,1)} async-done(((bf16[2048,256]{1,0:T(8,128)(2,1)}), bf16[2048,2048]{1,0:T(8,128)(2,1)}) %all-gather.23.cloned.1.call-update) | async-done | bytes 8388624 | tf_op jit(solution)/shard_map/all_gather | solution.py:116
  844.5 11.5 fusion.68
  856.4 83.6 %all-reduce.12.cloned.1.call-done = f32[512,2048]{1,0:T(8,128)} async-done(((f32[512,2048]{1,0:T(8,128)}), f32[512,2048]{1,0:T(8,128)}) %all-reduce.12.cloned.1.call-update) | async-done | bytes 4194320 | tf_op jit(solution)/shard_map/psum | solution.py:26
  939.9 4.0 fusion.76
  947.0 2.9 fusion.75
  950.0 12.0 fusion.87
  963.3 6.1 fusion.90
  969.7 85.5 %all-reduce.14.cloned.1.call-done = f32[512,2048]{1,0:T(8,128)} async-done(((f32[512,2048]{1,0:T(8,128)}), f32[512,2048]{1,0:T(8,128)}) %all-reduce.14.cloned.1.call-update) | async-done | bytes 4194320 | tf_op jit(solution)/shard_map/psum | solution.py:30
  1055.2 4.8 multiply_reduce_fusion
  1068.6 3.3 fusion.91
  1072.5 85.2 %all-reduce.16.cloned.1.call-done = f32[512,2048]{1,0:T(8,128)} async-done(((f32[512,2048]{1,0:T(8,128)}), f32[512,2048]{1,0:T(8,128)}) %all-reduce.16.cloned.1.call-update) | async-done | bytes 4194320 | tf_op jit(solution)/shard_map/psum | solution.py:30
  1157.7 4.7 multiply_reduce_fusion.1
  1183.2 8.6 convolution_bitcast_fusion.1
  1191.9 4.3 convolution_convert_fusion.3
  1201.5 7.2 fusion.4
  1208.8 4.9 convolution_convert_fusion.2
  1213.8 4.8 convolution_convert_fusion.4
  1218.7 12.4 convolution_convert_fusion
  1232.7 9.4 convolution_convert_fusion.1
  1244.1 7.1 convert_bitcast_fusion.1
  1251.2 7.2 convert_bitcast_fusion
  1260.7 16.9 all-reduce.18.cloned.1.call-done
  1277.6 3.3 fusion.70
  1283.1 38.6 %all-reduce = (bf16[4,2048]{1,0:T(4,128)(2,1)S(1)}, bf16[4,2048]{1,0:T(4,128)(2,1)S(1)}, bf16[3,2048]{1,0:T(4,128)(2,1)S(1)}, bf16[2048]{0:T(1024)(128)(2,1)S(1)}) all-reduce(bf16[4,2048]{1,0:T(4,128)(2,1)S(1)} %get-tuple-element.190, bf16[4,2048]{1,0:T(4,128)(2,1)S(1)} %get-tuple-element.191, ...), channel_id=1, replica_groups=mesh['dp'=8,'mp'=4] {'dp'}, use_global_device_ids=true, to_apply=%region_40.41 | all-reduce | flops 24576 | bytes 98304 | tf_op jit(solution)/shard_map/psum | solution.py:249
  1324.2 5.6 add_add_fusion.4
  1329.8 20.3 reduce-scatter.15.cloned.1.call-done
  1352.0 31.5 %reduce-scatter.9.cloned.1.call-done = bf16[256,1024]{1,0:T(8,128)(2,1)} async-done(((bf16[256,4096]{1,0:T(8,128)(2,1)}), bf16[256,1024]{1,0:T(8,128)(2,1)}) %reduce-scatter.9.cloned.1.call-update) | async-done | bytes 524304 | tf_op jit(solution)/shard_map/reduce_scatter | solution.py:207
  1385.6 70.2 %reduce-scatter.19.cloned.1.call-done = bf16[512,256]{1,0:T(8,128)(2,1)} async-done(((bf16[512,2048]{1,0:T(8,128)(2,1)}), bf16[512,256]{1,0:T(8,128)(2,1)}) %reduce-scatter.19.cloned.1.call-update) | async-done | bytes 262160 | tf_op jit(solution)/shard_map/reduce_scatter | solution.py:267
  1457.5 70.0 %reduce-scatter.13.cloned.1.call-done = bf16[512,256]{1,0:T(8,128)(2,1)} async-done(((bf16[512,2048]{1,0:T(8,128)(2,1)}), bf16[512,256]{1,0:T(8,128)(2,1)}) %reduce-scatter.13.cloned.1.call-update) | async-done | bytes 262160 | tf_op jit(solution)/shard_map/reduce_scatter | solution.py:258
  1529.3 148.7 %reduce-scatter.23.cloned.1.call-done = bf16[2048,256]{1,0:T(8,128)(2,1)} async-done(((bf16[2048,2048]{1,0:T(8,128)(2,1)}), bf16[2048,256]{1,0:T(8,128)(2,1)}) %reduce-scatter.23.cloned.1.call-update) | async-done | bytes 1048592 | tf_op jit(solution)/shard_map/reduce_scatter | solution.py:273
  1680.8 147.4 %reduce-scatter.21.cloned.1.call-done = bf16[256,2048]{1,0:T(8,128)(2,1)} async-done(((bf16[2048,2048]{1,0:T(8,128)(2,1)}), bf16[256,2048]{1,0:T(8,128)(2,1)}) %reduce-scatter.21.cloned.1.call-update) | async-done | bytes 1048592 | tf_op jit(solution)/shard_map/reduce_scatter | solution.py:270
  1830.9 118.5 %reduce-scatter.11.cloned.1.call-done = bf16[3,256,512]{1,2,0:T(8,128)(2,1)} async-done(((bf16[3,2048,512]{1,2,0:T(8,128)(2,1)}), bf16[3,256,512]{1,2,0:T(8,128)(2,1)}) %reduce-scatter.11.cloned.1.call-update) | async-done | bytes 786448 | tf_op jit(solution)/shard_map/reduce_scatter | solution.py:255
  1951.9 148.2 %reduce-scatter.17.cloned.1.call-done = bf16[2,512,512]{1,2,0:T(8,128)(2,1)} async-done(((bf16[2,4096,512]{1,2,0:T(8,128)(2,1)}), bf16[2,512,512]{1,2,0:T(8,128)(2,1)}) %reduce-scatter.17.cloned.1.call-update) | async-done | bytes 1048592 | tf_op jit(solution)/shard_map/reduce_scatter | solution.py:264
  (249 shorter events, 98.0 us)
Async XLA Ops:
  7.2 5.3 copy-start.6
  7.2 6.0 copy-start.42
  7.2 6.6 copy-start.40
  7.2 6.6 copy-start.41
  7.2 105.7 %all-gather.9.cloned.1.call-start = ((), (), s32[]{:S(2)}) async-start(), calls=%async_computation.8 | async-start | bytes 7077888 | tf_op jit(solution)/shard_map/all_gather | solution.py:110
  9.7 153.8 %all-gather.11.cloned.1.call-start = ((), (), s32[]{:S(2)}) async-start(), calls=%async_computation.9 | async-start | bytes 2359296 | tf_op jit(solution)/shard_map/all_gather | solution.py:111
  10.5 241.7 %all-reduce.8.cloned.1.call-start = ((), (), s32[]{:S(2)}) async-start(), calls=%async_computation.10 | async-start | bytes 8388608 | tf_op jit(solution)/shard_map/psum | solution.py:26
  12.5 107.0 %copy-start.38 = (f32[512]{0:T(512)}, f32[512]{0:T(512)S(1)}, u32[]{:S(2)}) copy-start(f32[512]{0:T(512)S(1)} %broadcast_multiply_fusion.3) | copy-start | bytes 6148
  13.8 105.7 %copy-start.43 = (f32[512]{0:T(512)}, f32[512]{0:T(512)S(1)}, u32[]{:S(2)}) copy-start(f32[512]{0:T(512)S(1)} %fusion.58) | copy-start | bytes 6148
  13.8 105.7 %copy-start.36 = (f32[1,2048]{1,0:T(1,128)}, f32[1,2048]{1,0:T(1,128)S(1)}, u32[]{:S(2)}) copy-start(f32[1,2048]{1,0:T(1,128)S(1)} %get-tuple-element.171) | copy-start | bytes 24580
  13.9 105.6 %copy-start.48 = (f32[1,2048]{1,0:T(1,128)}, f32[1,2048]{1,0:T(1,128)S(1)}, u32[]{:S(2)}) copy-start(f32[1,2048]{1,0:T(1,128)S(1)} %get-tuple-element.175) | copy-start | bytes 24580
  124.3 39.2 %copy-start.32 = (bf16[4,128,512]{2,1,0:T(8,128)(2,1)}, bf16[4,128,512]{2,1,0:T(8,128)(2,1)S(1)}, u32[]{:S(2)}) copy-start(bf16[4,128,512]{2,1,0:T(8,128)(2,1)S(1)} %fusion.45) | copy-start | bytes 1572868
  168.4 3.9 copy-start.45
  168.4 4.0 copy-start.50
  168.4 135.1 %all-gather.17.cloned.1.call-start = ((), (), s32[]{:S(2)}) async-start(), calls=%async_computation.13 | async-start | bytes 2359296 | tf_op jit(solution)/shard_map/all_gather | solution.py:112
  169.0 157.0 %all-gather.15.cloned.1.call-start = ((), (), s32[]{:S(2)}) async-start(), calls=%async_computation.12 | async-start | bytes 2621440 | tf_op jit(solution)/shard_map/all_gather | solution.py:119
  169.6 283.9 %all-gather.13.cloned.1.call-start = ((), (), s32[]{:S(2)}) async-start(), calls=%async_computation.11 | async-start | bytes 9437184 | tf_op jit(solution)/shard_map/all_gather | solution.py:113
  171.0 333.1 %all-gather.19.cloned.1.call-start = ((), (), s32[]{:S(2)}) async-start(), calls=%async_computation.14 | async-start | bytes 2359296 | tf_op jit(solution)/shard_map/all_gather | solution.py:114
  171.7 421.0 %all-reduce.10.cloned.1.call-start = ((), (), s32[]{:S(2)}) async-start(), calls=%async_computation.15 | async-start | bytes 8388608 | tf_op jit(solution)/shard_map/psum | solution.py:26
  257.8 48.5 %copy-start.28 = (bf16[512,2048]{1,0:T(8,128)(2,1)}, bf16[512,2048]{1,0:T(8,128)(2,1)S(1)}, u32[]{:S(2)}) copy-start(bf16[512,2048]{1,0:T(8,128)(2,1)S(1)} %add_convert_fusion.2) | copy-start | bytes 6291460
  306.4 153.5 %copy-start.26 = (bf16[512,512]{0,1:T(8,128)(2,1)}, bf16[512,512]{0,1:T(8,128)(2,1)S(1)}, u32[]{:S(2)}) copy-start(bf16[512,512]{0,1:T(8,128)(2,1)S(1)} %convolution_convert_fusion.9) | copy-start | bytes 1572868
  461.3 47.6 %copy-start.34 = (bf16[4,128,512]{2,1,0:T(8,128)(2,1)}, bf16[4,128,512]{2,1,0:T(8,128)(2,1)S(1)}, u32[]{:S(2)}) copy-start(bf16[4,128,512]{2,1,0:T(8,128)(2,1)S(1)} %convolution_convert_fusion.8) | copy-start | bytes 1572868
  508.9 210.6 %all-gather.21.cloned.1.call-start = ((), (), s32[]{:S(2)}) async-start(), calls=%async_computation.16 | async-start | bytes 9437184 | tf_op jit(solution)/shard_map/all_gather | solution.py:115
  509.7 334.9 %all-gather.23.cloned.1.call-start = ((), (), s32[]{:S(2)}) async-start(), calls=%async_computation.17 | async-start | bytes 9437184 | tf_op jit(solution)/shard_map/all_gather | solution.py:116
  510.2 429.7 %all-reduce.12.cloned.1.call-start = ((), (), s32[]{:S(2)}) async-start(), calls=%async_computation.18 | async-start | bytes 8388608 | tf_op jit(solution)/shard_map/psum | solution.py:26
  719.5 125.0 %copy-start.51 = (f32[2048]{0:T(1024)S(1)}, f32[2048]{0:T(1024)}, u32[]{:S(2)}) copy-start(f32[2048]{0:T(1024)} %param.30) | copy-start | bytes 24580
  856.1 199.1 %all-reduce.14.cloned.1.call-start = ((), (), s32[]{:S(2)}) async-start(), calls=%async_computation.19 | async-start | bytes 8388608 | tf_op jit(solution)/shard_map/psum | solution.py:30
  947.0 16.3 slice-start
  949.9 12.0 copy-start.10
  949.9 13.3 slice-start.1
  969.4 188.3 %all-reduce.16.cloned.1.call-start = ((), (), s32[]{:S(2)}) async-start(), calls=%async_computation.20 | async-start | bytes 8388608 | tf_op jit(solution)/shard_map/psum | solution.py:30
  1055.2 4.8 copy-start.5
  1055.2 5.9 copy-start.15
  1071.9 205.7 %all-reduce.18.cloned.1.call-start = ((), (), s32[]{:S(2)}) async-start(), calls=%async_computation.21 | async-start | bytes 8388608 | tf_op jit(solution)/shard_map/psum | solution.py:30
  1157.7 4.7 copy-start.1
  1157.7 5.9 copy-start.14
  1166.4 3.9 copy-start.3
  1191.8 158.3 %reduce-scatter.15.cloned.1.call-start = ((), (), s32[]{:S(2)}) async-start(), calls=%async_computation.25 | async-start | bytes 2359296 | tf_op jit(solution)/shard_map/reduce_scatter | solution.py:261
  1196.2 187.2 %reduce-scatter.9.cloned.1.call-start = ((), (), s32[]{:S(2)}) async-start(), calls=%async_computation.22 | async-start | bytes 2621440 | tf_op jit(solution)/shard_map/reduce_scatter | solution.py:207
  1201.5 7.3 copy-start.35
  1208.7 5.0 copy-start.33
  1208.7 247.0 %reduce-scatter.19.cloned.1.call-start = ((), (), s32[]{:S(2)}) async-start(), calls=%async_computation.27 | async-start | bytes 2359296 | tf_op jit(solution)/shard_map/reduce_scatter | solution.py:267
  1213.7 313.9 %reduce-scatter.13.cloned.1.call-start = ((), (), s32[]{:S(2)}) async-start(), calls=%async_computation.24 | async-start | bytes 2359296 | tf_op jit(solution)/shard_map/reduce_scatter | solution.py:258
  1218.6 459.5 %reduce-scatter.23.cloned.1.call-start = ((), (), s32[]{:S(2)}) async-start(), calls=%async_computation.29 | async-start | bytes 9437184 | tf_op jit(solution)/shard_map/reduce_scatter | solution.py:273
  1231.1 597.1 %reduce-scatter.21.cloned.1.call-start = ((), (), s32[]{:S(2)}) async-start(), calls=%async_computation.28 | async-start | bytes 9437184 | tf_op jit(solution)/shard_map/reduce_scatter | solution.py:270
  1242.2 707.2 %reduce-scatter.11.cloned.1.call-start = ((), (), s32[]{:S(2)}) async-start(), calls=%async_computation.23 | async-start | bytes 7077888 | tf_op jit(solution)/shard_map/reduce_scatter | solution.py:255
  1251.2 849.0 %reduce-scatter.17.cloned.1.call-start = ((), (), s32[]{:S(2)}) async-start(), calls=%async_computation.26 | async-start | bytes 9437184 | tf_op jit(solution)/shard_map/reduce_scatter | solution.py:264
  1258.5 22.4 %copy-start.47 = (f32[512]{0:T(512)S(1)}, f32[512]{0:T(512)}, u32[]{:S(2)}) copy-start(f32[512]{0:T(512)} %copy-done.46) | copy-start | bytes 6148
  (31 other events, 58.3 us)
Sparse Core Ops, SparseCore 0:
  10.6 102.1 all-gather.8
  114.9 48.5 all-gather.10
  168.5 83.6 all-reduce.7
  254.2 49.2 all-gather.16
  304.9 21.0 all-gather.14
  328.5 124.9 all-gather.12
  455.5 48.5 all-gather.18
  509.0 83.6 all-reduce.9
  594.9 124.6 all-gather.20
  721.4 123.1 all-gather.22
  856.2 83.6 all-reduce.11
  969.5 85.6 all-reduce.13
  1072.1 85.6 all-reduce.15
  1191.9 85.6 all-reduce.17
  1281.5 68.5 reduce-scatter.14
  1353.1 30.2 reduce-scatter.8
  1386.8 68.8 reduce-scatter.18
  1459.7 67.8 reduce-scatter.12
  1531.2 146.8 reduce-scatter.22
  1681.6 146.5 reduce-scatter.20
  1831.8 117.5 reduce-scatter.10
  1953.0 147.0 reduce-scatter.16
where the time goes:
time: 2120 us; the launch traced here: 2110 us
  waiting for transfers between devices  1800 us (85%)
  matrix products  151 us (7%)
  other arithmetic  65.1 us (3%)
  blocking collectives  38.6 us (2%)
  local copies, waits for them, and re-layouts  36.8 us (2%)
    psum x3, waiting for transfers between devices, heads_sum(): return lax.psum(partial_value, 'mp')  246 us
    psum x3, waiting for transfers between devices, input_sum(): return lax.psum(partial_value, 'mp')  188 us
    reduce_scatter x1, waiting for transfers between devices, on_device(): lax.psum_scatter(grad_down.astype(jnp.bfloat16), 'dp', scatter_dimension=...  149 us
    reduce_scatter x1, waiting for transfers between devices, on_device(): lax.psum_scatter(grad_ckv.astype(jnp.bfloat16), 'dp', scatter_dimension=1...  148 us
    reduce_scatter x1, waiting for transfers between devices, on_device(): lax.psum_scatter(grad_up.astype(jnp.bfloat16), 'dp', scatter_dimension=0,...  147 us
    all_gather x1, waiting for transfers between devices, on_device(): lax.all_gather(c_kv, 'dp', axis=1, tiled=True)  127 us
    all_gather x1, waiting for transfers between devices, on_device(): lax.all_gather(w_up, 'dp', axis=0, tiled=True)  120 us
    reduce_scatter x1, waiting for transfers between devices, on_device(): lax.psum_scatter(grad_qkv.astype(jnp.bfloat16), 'dp', scatter_dimension=1...  118 us
  transfers between devices with their start and end apart: 22, of which 22 were waited for; matrix products, arithmetic and copies ran while one was open for 7% of the time, Pallas kernels for 0%

commit v1 on v0

--- a/solution.py
+++ b/solution.py
@@ -6,6 +6,23 @@
 HD = 128
 eps = 1e-05
 masked = -1e30
+
+
+def laid_out(parts, dim):
+    parts = jnp.moveaxis(parts, 0, dim)
+    lengths = parts.shape
+    return parts.reshape(*lengths[:dim], lengths[dim] * lengths[dim + 1], *lengths[dim + 2 :])
+
+
+def collect(x, axis, dim):
+    peers = lax.axis_size(axis)
+    right = [(i, (i + 1) % peers) for i in range(peers)]
+    pieces = [x]
+    while len(pieces) < peers:
+        pieces.append(lax.ppermute(pieces[-1], axis, right))
+    place = lax.axis_index(axis)
+    pieces = jnp.stack(pieces)[(place - jnp.arange(peers)) % peers]
+    return laid_out(pieces, dim)
 
 
 def normalize(values, gain, shift):
@@ -107,7 +124,7 @@
     length = image_seg.shape[1]
     text_len = text_seg.shape[1]
     gathered = (
-        lax.all_gather(w_qkv, "dp", axis=1, tiled=True),
+        collect(w_qkv, "dp", 1),
         lax.all_gather(w_out, "dp", axis=1, tiled=True),
         lax.all_gather(c_q, "dp", axis=0, tiled=True),
         lax.all_gather(c_kv, "dp", axis=1, tiled=True),

time: 2120 us -> 2140 us (level)
    ppermute x0 -> x7, waiting for transfers between devices: none -> 142 us  [collect(): pieces.append(lax.ppermute(pieces[-1], axis, right))]
    all_gather x1 -> x0, waiting for transfers between devices: 99 us -> none  [on_device(): lax.all_gather(w_qkv, 'dp', axis=1, tiled=True)]
    all_gather x1, waiting for transfers between devices: 39.2 us -> 0.02 us  [on_device(): lax.all_gather(w_out, 'dp', axis=1, tiled=True)]
  transfers between devices with their start and end apart: 22 -> 28, of which waited for: 22 -> 27; matrix products, arithmetic and copies ran while one was open for 7% -> 7% of each run, Pallas kernels for 0% -> 0%
where the time goes in v1:
time: 2140 us; the launch traced here: 2130 us
  waiting for transfers between devices  1800 us (84%)
  matrix products  149 us (7%)
  other arithmetic  66.6 us (3%)
  local copies, waits for them, and re-layouts  53.5 us (2%)
  blocking collectives  38.9 us (2%)
    psum x3, waiting for transfers between devices, heads_sum(): return lax.psum(partial_value, 'mp')  244 us
    psum x3, waiting for transfers between devices, input_sum(): return lax.psum(partial_value, 'mp')  188 us
    reduce_scatter x1, waiting for transfers between devices, on_device(): lax.psum_scatter(grad_down.astype(jnp.bfloat16), 'dp', scatter_dimension=...  149 us
    reduce_scatter x1, waiting for transfers between devices, on_device(): lax.psum_scatter(grad_ckv.astype(jnp.bfloat16), 'dp', scatter_dimension=1...  148 us
    reduce_scatter x1, waiting for transfers between devices, on_device(): lax.psum_scatter(grad_up.astype(jnp.bfloat16), 'dp', scatter_dimension=0,...  148 us
    ppermute x7, waiting for transfers between devices, collect(): pieces.append(lax.ppermute(pieces[-1], axis, right))  142 us
    all_gather x1, waiting for transfers between devices, on_device(): lax.all_gather(c_kv, 'dp', axis=1, tiled=True)  127 us
    all_gather x1, waiting for transfers between devices, on_device(): lax.all_gather(w_up, 'dp', axis=0, tiled=True)  120 us
  transfers between devices with their start and end apart: 28, of which 27 were waited for; matrix products, arithmetic and copies ran while one was open for 7% of the time, Pallas kernels for 0%

profile of v1, /device:TPU:0, one launch (start us, length us, event | category | flops | bytes accessed | tf_op | source)
XLA Modules:
  0.0 2131.2 jit_solution(13360007467871900228)
XLA Ops:
  10.3 20.8 collective-permute-done
  31.2 27.5 %collective-permute-done.1 = bf16[3,256,512]{2,1,0:T(8,128)(2,1)S(1)} collective-permute-done((bf16[3,256,512]{2,1,0:T(8,128)(2,1)S(1)}, bf16[3,256,512]{2,1,0:T(8,128)(2,1)S(1)}, u32[]{:S(2)}, u32[]{:S(2)}) %collective-permute-start.1) | collective-permute-done | bytes 786464 | tf_op jit(solution)/shard_map/ppermute | solution.py:22
  62.9 15.1 collective-permute-done.2
  78.4 36.4 %collective-permute-done.3 = bf16[3,256,512]{2,1,0:T(8,128)(2,1)S(1)} collective-permute-done((bf16[3,256,512]{2,1,0:T(8,128)(2,1)}, bf16[3,256,512]{2,1,0:T(8,128)(2,1)S(1)}, u32[]{:S(2)}, u32[]{:S(2)}) %collective-permute-start.3) | collective-permute-done | bytes 786464 | tf_op jit(solution)/shard_map/ppermute | solution.py:22
  115.8 16.7 collective-permute-done.4
  136.4 13.8 collective-permute-done.5
  153.1 11.8 collective-permute-done.6
  165.8 6.4 gather_fusion
  185.3 4.9 fusion.90
  193.9 78.6 %all-reduce.8.cloned.1.call-done = f32[512,2048]{1,0:T(8,128)} async-done(((f32[512,2048]{1,0:T(8,128)}), f32[512,2048]{1,0:T(8,128)}) %all-reduce.8.cloned.1.call-update) | async-done | bytes 4194320 | tf_op jit(solution)/shard_map/psum | solution.py:43
  278.1 45.8 %all-gather.14.cloned.1.call-done = bf16[2048,512]{1,0:T(8,128)(2,1)} async-done(((bf16[256,512]{1,0:T(8,128)(2,1)}), bf16[2048,512]{1,0:T(8,128)(2,1)}) %all-gather.14.cloned.1.call-update) | async-done | bytes 2097168 | tf_op jit(solution)/shard_map/all_gather | solution.py:129
  326.8 19.6 all-gather.12.cloned.1.call-done
  346.4 127.4 %all-gather.10.cloned.1.call-done = bf16[2,4096,512]{1,2,0:T(8,128)(2,1)} async-done(((bf16[2,512,512]{1,2,0:T(8,128)(2,1)}), bf16[2,4096,512]{1,2,0:T(8,128)(2,1)}) %all-gather.10.cloned.1.call-update) | async-done | bytes 8388624 | tf_op jit(solution)/shard_map/all_gather | solution.py:130
  473.9 6.3 fusion.46
  481.7 42.6 %all-gather.16.cloned.1.call-done = bf16[512,2048]{1,0:T(8,128)(2,1)} async-done(((bf16[512,256]{1,0:T(8,128)(2,1)}), bf16[512,2048]{1,0:T(8,128)(2,1)}) %all-gather.16.cloned.1.call-update) | async-done | bytes 2097168 | tf_op jit(solution)/shard_map/all_gather | solution.py:131
  524.3 4.9 fusion.91
  531.0 82.1 %all-reduce.10.cloned.1.call-done = f32[512,2048]{1,0:T(8,128)} async-done(((f32[512,2048]{1,0:T(8,128)}), f32[512,2048]{1,0:T(8,128)}) %all-reduce.10.cloned.1.call-update) | async-done | bytes 4194320 | tf_op jit(solution)/shard_map/psum | solution.py:43
  619.6 120.2 %all-gather.18.cloned.1.call-done = bf16[2048,2048]{1,0:T(8,128)(2,1)} async-done(((bf16[256,2048]{1,0:T(8,128)(2,1)}), bf16[2048,2048]{1,0:T(8,128)(2,1)}) %all-gather.18.cloned.1.call-update) | async-done | bytes 8388624 | tf_op jit(solution)/shard_map/all_gather | solution.py:132
  739.8 11.2 fusion.71
  751.0 114.0 %all-gather.20.cloned.1.call-done = bf16[2048,2048]{1,0:T(8,128)(2,1)} async-done(((bf16[2048,256]{1,0:T(8,128)(2,1)}), bf16[2048,2048]{1,0:T(8,128)(2,1)}) %all-gather.20.cloned.1.call-update) | async-done | bytes 8388624 | tf_op jit(solution)/shard_map/all_gather | solution.py:133
  865.0 11.6 fusion.70
  876.9 83.5 %all-reduce.12.cloned.1.call-done = f32[512,2048]{1,0:T(8,128)} async-done(((f32[512,2048]{1,0:T(8,128)}), f32[512,2048]{1,0:T(8,128)}) %all-reduce.12.cloned.1.call-update) | async-done | bytes 4194320 | tf_op jit(solution)/shard_map/psum | solution.py:43
  970.5 12.0 fusion.89
  983.8 6.1 fusion.92
  990.4 85.2 %all-reduce.14.cloned.1.call-done = f32[512,2048]{1,0:T(8,128)} async-done(((f32[512,2048]{1,0:T(8,128)}), f32[512,2048]{1,0:T(8,128)}) %all-reduce.14.cloned.1.call-update) | async-done | bytes 4194320 | tf_op jit(solution)/shard_map/psum | solution.py:47
  1075.7 4.7 multiply_reduce_fusion
  1092.7 85.5 %all-reduce.16.cloned.1.call-done = f32[512,2048]{1,0:T(8,128)} async-done(((f32[512,2048]{1,0:T(8,128)}), f32[512,2048]{1,0:T(8,128)}) %all-reduce.16.cloned.1.call-update) | async-done | bytes 4194320 | tf_op jit(solution)/shard_map/psum | solution.py:47
  1178.3 4.6 multiply_reduce_fusion.1
  1203.7 8.7 convolution_bitcast_fusion.1
  1212.5 4.3 convolution_convert_fusion.3
  1222.2 7.2 fusion.4
  1229.4 5.0 convolution_convert_fusion.2
  1234.5 4.9 convolution_convert_fusion.4
  1239.4 12.4 convolution_convert_fusion
  1253.5 9.5 convolution_convert_fusion.1
  1264.8 7.1 convert_bitcast_fusion.1
  1272.0 7.2 convert_bitcast_fusion
  1281.4 16.8 all-reduce.18.cloned.1.call-done
  1303.7 38.9 %all-reduce = (bf16[4,2048]{1,0:T(4,128)(2,1)S(1)}, bf16[4,2048]{1,0:T(4,128)(2,1)S(1)}, bf16[3,2048]{1,0:T(4,128)(2,1)S(1)}, bf16[2048]{0:T(1024)(128)(2,1)S(1)}) all-reduce(bf16[4,2048]{1,0:T(4,128)(2,1)S(1)} %get-tuple-element.218, bf16[4,2048]{1,0:T(4,128)(2,1)S(1)} %get-tuple-element.219, ...), channel_id=1, replica_groups=mesh['dp'=8,'mp'=4] {'dp'}, use_global_device_ids=true, to_apply=%region_40.41 | all-reduce | flops 24576 | bytes 98304 | tf_op jit(solution)/shard_map/psum | solution.py:266
  1345.1 5.6 add_add_fusion.4
  1350.7 20.3 reduce-scatter.15.cloned.1.call-done
  1372.8 31.3 %reduce-scatter.9.cloned.1.call-done = bf16[256,1024]{1,0:T(8,128)(2,1)} async-done(((bf16[256,4096]{1,0:T(8,128)(2,1)}), bf16[256,1024]{1,0:T(8,128)(2,1)}) %reduce-scatter.9.cloned.1.call-update) | async-done | bytes 524304 | tf_op jit(solution)/shard_map/reduce_scatter | solution.py:224
  1406.2 70.5 %reduce-scatter.19.cloned.1.call-done = bf16[512,256]{1,0:T(8,128)(2,1)} async-done(((bf16[512,2048]{1,0:T(8,128)(2,1)}), bf16[512,256]{1,0:T(8,128)(2,1)}) %reduce-scatter.19.cloned.1.call-update) | async-done | bytes 262160 | tf_op jit(solution)/shard_map/reduce_scatter | solution.py:284
  1478.5 70.4 %reduce-scatter.13.cloned.1.call-done = bf16[512,256]{1,0:T(8,128)(2,1)} async-done(((bf16[512,2048]{1,0:T(8,128)(2,1)}), bf16[512,256]{1,0:T(8,128)(2,1)}) %reduce-scatter.13.cloned.1.call-update) | async-done | bytes 262160 | tf_op jit(solution)/shard_map/reduce_scatter | solution.py:275
  1550.7 148.6 %reduce-scatter.23.cloned.1.call-done = bf16[2048,256]{1,0:T(8,128)(2,1)} async-done(((bf16[2048,2048]{1,0:T(8,128)(2,1)}), bf16[2048,256]{1,0:T(8,128)(2,1)}) %reduce-scatter.23.cloned.1.call-update) | async-done | bytes 1048592 | tf_op jit(solution)/shard_map/reduce_scatter | solution.py:290
  1702.0 147.5 %reduce-scatter.21.cloned.1.call-done = bf16[256,2048]{1,0:T(8,128)(2,1)} async-done(((bf16[2048,2048]{1,0:T(8,128)(2,1)}), bf16[256,2048]{1,0:T(8,128)(2,1)}) %reduce-scatter.21.cloned.1.call-update) | async-done | bytes 1048592 | tf_op jit(solution)/shard_map/reduce_scatter | solution.py:287
  1852.3 118.2 %reduce-scatter.11.cloned.1.call-done = bf16[3,256,512]{1,2,0:T(8,128)(2,1)} async-done(((bf16[3,2048,512]{1,2,0:T(8,128)(2,1)}), bf16[3,256,512]{1,2,0:T(8,128)(2,1)}) %reduce-scatter.11.cloned.1.call-update) | async-done | bytes 786448 | tf_op jit(solution)/shard_map/reduce_scatter | solution.py:272
  1973.1 148.2 %reduce-scatter.17.cloned.1.call-done = bf16[2,512,512]{1,2,0:T(8,128)(2,1)} async-done(((bf16[2,4096,512]{1,2,0:T(8,128)(2,1)}), bf16[2,512,512]{1,2,0:T(8,128)(2,1)}) %reduce-scatter.17.cloned.1.call-update) | async-done | bytes 1048592 | tf_op jit(solution)/shard_map/reduce_scatter | solution.py:281
  (275 shorter events, 133.5 us)
Async XLA Ops:
  7.2 107.6 %copy-start.32 = (bf16[3,256,512]{2,1,0:T(8,128)(2,1)S(1)}, bf16[3,256,512]{2,1,0:T(8,128)(2,1)}, u32[]{:S(2)}) copy-start(bf16[3,256,512]{2,1,0:T(8,128)(2,1)} %param.20) | copy-start | bytes 2359300
  7.2 70.9 %copy-start.44 = (s32[1,512]{1,0:T(1,128)S(1)}, s32[1,512]{1,0:T(1,128)}, u32[]{:S(2)}) copy-start(s32[1,512]{1,0:T(1,128)} %param.18) | copy-start | bytes 6148
  7.2 71.1 %copy-start.42 = (f32[4,2048]{1,0:T(4,128)S(1)}, f32[4,2048]{1,0:T(4,128)}, u32[]{:S(2)}) copy-start(f32[4,2048]{1,0:T(4,128)} %param.27) | copy-start | bytes 98308
  7.2 108.5 %copy-start.43 = (f32[4,2048]{1,0:T(4,128)S(1)}, f32[4,2048]{1,0:T(4,128)}, u32[]{:S(2)}) copy-start(f32[4,2048]{1,0:T(4,128)} %param.28) | copy-start | bytes 98308
  7.2 177.3 %all-gather.8.cloned.1.call-start = ((), (), s32[]{:S(2)}) async-start(), calls=%async_computation.8 | async-start | bytes 2359296 | tf_op jit(solution)/shard_map/all_gather | solution.py:128
  7.3 23.8 %collective-permute-start = (bf16[3,256,512]{2,1,0:T(8,128)(2,1)}, bf16[3,256,512]{2,1,0:T(8,128)(2,1)S(1)}, u32[]{:S(2)}, u32[]{:S(2)}) collective-permute-start(bf16[3,256,512]{2,1,0:T(8,128)(2,1)} %param.20), channel_id=1, source_target_pairs={{0,4},{4,8},{8,12},{12,16},{16,20},{20,24},{24,28},{28,0},{1,5},{5... | collective-permute-start | bytes 2359304 | tf_op jit(solution)/shard_map/ppermute | solution.py:22
  31.1 27.6 %collective-permute-start.1 = (bf16[3,256,512]{2,1,0:T(8,128)(2,1)S(1)}, bf16[3,256,512]{2,1,0:T(8,128)(2,1)S(1)}, u32[]{:S(2)}, u32[]{:S(2)}) collective-permute-start(bf16[3,256,512]{2,1,0:T(8,128)(2,1)S(1)} %collective-permute-done), channel_id=1, source_target_pairs={{0,4},{4,8},{8,12},{12,16},{16,20},{20,24},{24,28},{28,0},{1,5},{5... | collective-permute-start | bytes 2359304 | tf_op jit(solution)/shard_map/ppermute | solution.py:22
  31.1 241.3 %all-reduce.8.cloned.1.call-start = ((), (), s32[]{:S(2)}) async-start(), calls=%async_computation.9 | async-start | bytes 8388608 | tf_op jit(solution)/shard_map/psum | solution.py:43
  58.7 19.4 collective-permute-start.2
  60.6 115.2 %copy-start.40 = (f32[512]{0:T(512)}, f32[512]{0:T(512)S(1)}, u32[]{:S(2)}) copy-start(f32[512]{0:T(512)S(1)} %broadcast_multiply_fusion.3) | copy-start | bytes 6148
  62.9 15.2 copy-start.48
  62.9 112.9 %copy-start.45 = (f32[512]{0:T(512)}, f32[512]{0:T(512)S(1)}, u32[]{:S(2)}) copy-start(f32[512]{0:T(512)S(1)} %fusion.58) | copy-start | bytes 6148
  78.1 36.7 %collective-permute-start.3 = (bf16[3,256,512]{2,1,0:T(8,128)(2,1)}, bf16[3,256,512]{2,1,0:T(8,128)(2,1)S(1)}, u32[]{:S(2)}, u32[]{:S(2)}) collective-permute-start(bf16[3,256,512]{2,1,0:T(8,128)(2,1)} %collective-permute-done.2), channel_id=1, source_target_pairs={{0,4},{4,8},{8,12},{12,16},{16,20},{20,24},{24,28},{28,0},{1,5},{5... | collective-permute-start | bytes 2359304 | tf_op jit(solution)/shard_map/ppermute | solution.py:22
  78.4 97.4 %copy-start.38 = (f32[1,2048]{1,0:T(1,128)}, f32[1,2048]{1,0:T(1,128)S(1)}, u32[]{:S(2)}) copy-start(f32[1,2048]{1,0:T(1,128)S(1)} %get-tuple-element.199) | copy-start | bytes 24580
  114.8 17.7 collective-permute-start.4
  115.8 60.1 %copy-start.50 = (f32[1,2048]{1,0:T(1,128)}, f32[1,2048]{1,0:T(1,128)S(1)}, u32[]{:S(2)}) copy-start(f32[1,2048]{1,0:T(1,128)S(1)} %get-tuple-element.203) | copy-start | bytes 24580
  132.5 17.7 collective-permute-start.5
  150.2 14.7 collective-permute-start.6
  190.2 133.7 %all-gather.14.cloned.1.call-start = ((), (), s32[]{:S(2)}) async-start(), calls=%async_computation.12 | async-start | bytes 2359296 | tf_op jit(solution)/shard_map/all_gather | solution.py:129
  190.9 155.5 %all-gather.12.cloned.1.call-start = ((), (), s32[]{:S(2)}) async-start(), calls=%async_computation.11 | async-start | bytes 2621440 | tf_op jit(solution)/shard_map/all_gather | solution.py:136
  191.5 282.4 %all-gather.10.cloned.1.call-start = ((), (), s32[]{:S(2)}) async-start(), calls=%async_computation.10 | async-start | bytes 9437184 | tf_op jit(solution)/shard_map/all_gather | solution.py:130
  192.9 331.4 %all-gather.16.cloned.1.call-start = ((), (), s32[]{:S(2)}) async-start(), calls=%async_computation.13 | async-start | bytes 2359296 | tf_op jit(solution)/shard_map/all_gather | solution.py:131
  193.5 419.5 %all-reduce.10.cloned.1.call-start = ((), (), s32[]{:S(2)}) async-start(), calls=%async_computation.14 | async-start | bytes 8388608 | tf_op jit(solution)/shard_map/psum | solution.py:43
  278.1 48.7 %copy-start.29 = (bf16[512,2048]{1,0:T(8,128)(2,1)}, bf16[512,2048]{1,0:T(8,128)(2,1)S(1)}, u32[]{:S(2)}) copy-start(bf16[512,2048]{1,0:T(8,128)(2,1)S(1)} %add_convert_fusion.2) | copy-start | bytes 6291460
  326.8 153.5 %copy-start.27 = (bf16[512,512]{0,1:T(8,128)(2,1)}, bf16[512,512]{0,1:T(8,128)(2,1)S(1)}, u32[]{:S(2)}) copy-start(bf16[512,512]{0,1:T(8,128)(2,1)S(1)} %convolution_convert_fusion.9) | copy-start | bytes 1572868
  481.7 47.5 %copy-start.36 = (bf16[4,128,512]{2,1,0:T(8,128)(2,1)}, bf16[4,128,512]{2,1,0:T(8,128)(2,1)S(1)}, u32[]{:S(2)}) copy-start(bf16[4,128,512]{2,1,0:T(8,128)(2,1)S(1)} %convolution_convert_fusion.8) | copy-start | bytes 1572868
  529.2 210.6 %all-gather.18.cloned.1.call-start = ((), (), s32[]{:S(2)}) async-start(), calls=%async_computation.15 | async-start | bytes 9437184 | tf_op jit(solution)/shard_map/all_gather | solution.py:132
  530.0 335.0 %all-gather.20.cloned.1.call-start = ((), (), s32[]{:S(2)}) async-start(), calls=%async_computation.16 | async-start | bytes 9437184 | tf_op jit(solution)/shard_map/all_gather | solution.py:133
  530.7 429.7 %all-reduce.12.cloned.1.call-start = ((), (), s32[]{:S(2)}) async-start(), calls=%async_computation.17 | async-start | bytes 8388608 | tf_op jit(solution)/shard_map/psum | solution.py:43
  739.8 125.2 %copy-start.53 = (f32[2048]{0:T(1024)S(1)}, f32[2048]{0:T(1024)}, u32[]{:S(2)}) copy-start(f32[2048]{0:T(1024)} %param.30) | copy-start | bytes 24580
  876.6 199.1 %all-reduce.14.cloned.1.call-start = ((), (), s32[]{:S(2)}) async-start(), calls=%async_computation.18 | async-start | bytes 8388608 | tf_op jit(solution)/shard_map/psum | solution.py:47
  967.5 16.3 slice-start
  970.5 12.0 copy-start.10
  970.5 13.3 slice-start.1
  989.9 188.3 %all-reduce.16.cloned.1.call-start = ((), (), s32[]{:S(2)}) async-start(), calls=%async_computation.19 | async-start | bytes 8388608 | tf_op jit(solution)/shard_map/psum | solution.py:47
  1075.7 5.9 copy-start.15
  1092.5 205.7 %all-reduce.18.cloned.1.call-start = ((), (), s32[]{:S(2)}) async-start(), calls=%async_computation.20 | async-start | bytes 8388608 | tf_op jit(solution)/shard_map/psum | solution.py:47
  1178.2 5.9 copy-start.14
  1212.4 158.6 %reduce-scatter.15.cloned.1.call-start = ((), (), s32[]{:S(2)}) async-start(), calls=%async_computation.24 | async-start | bytes 2359296 | tf_op jit(solution)/shard_map/reduce_scatter | solution.py:278
  1216.8 187.3 %reduce-scatter.9.cloned.1.call-start = ((), (), s32[]{:S(2)}) async-start(), calls=%async_computation.21 | async-start | bytes 2621440 | tf_op jit(solution)/shard_map/reduce_scatter | solution.py:224
  1222.2 7.3 copy-start.37
  1229.4 247.3 %reduce-scatter.19.cloned.1.call-start = ((), (), s32[]{:S(2)}) async-start(), calls=%async_computation.26 | async-start | bytes 2359296 | tf_op jit(solution)/shard_map/reduce_scatter | solution.py:284
  1234.4 314.5 %reduce-scatter.13.cloned.1.call-start = ((), (), s32[]{:S(2)}) async-start(), calls=%async_computation.23 | async-start | bytes 2359296 | tf_op jit(solution)/shard_map/reduce_scatter | solution.py:275
  1239.4 459.9 %reduce-scatter.23.cloned.1.call-start = ((), (), s32[]{:S(2)}) async-start(), calls=%async_computation.28 | async-start | bytes 9437184 | tf_op jit(solution)/shard_map/reduce_scatter | solution.py:290
  1251.8 597.6 %reduce-scatter.21.cloned.1.call-start = ((), (), s32[]{:S(2)}) async-start(), calls=%async_computation.27 | async-start | bytes 9437184 | tf_op jit(solution)/shard_map/reduce_scatter | solution.py:287
  1263.0 707.5 %reduce-scatter.11.cloned.1.call-start = ((), (), s32[]{:S(2)}) async-start(), calls=%async_computation.22 | async-start | bytes 7077888 | tf_op jit(solution)/shard_map/reduce_scatter | solution.py:272
  1272.0 849.3 %reduce-scatter.17.cloned.1.call-start = ((), (), s32[]{:S(2)}) async-start(), calls=%async_computation.25 | async-start | bytes 9437184 | tf_op jit(solution)/shard_map/reduce_scatter | solution.py:281
  1279.2 22.3 %copy-start.49 = (f32[512]{0:T(512)S(1)}, f32[512]{0:T(512)}, u32[]{:S(2)}) copy-start(f32[512]{0:T(512)} %copy-done.48) | copy-start | bytes 6148
  (39 other events, 91.7 us)
Sparse Core Ops, SparseCore 0:
  31.3 81.3 all-gather.7
  190.3 82.1 all-reduce.7
  274.6 49.2 all-gather.13
  325.3 21.0 all-gather.11
  348.9 124.9 all-gather.9
  475.8 48.5 all-gather.15
  529.3 83.6 all-reduce.9
  615.1 124.6 all-gather.17
  741.8 123.1 all-gather.19
  876.7 83.6 all-reduce.11
  990.0 85.6 all-reduce.13
  1092.6 85.6 all-reduce.15
  1212.5 85.6 all-reduce.17
  1302.2 68.7 reduce-scatter.14
  1373.9 30.1 reduce-scatter.8
  1407.5 69.1 reduce-scatter.18
  1480.6 68.2 reduce-scatter.12
  1552.4 146.8 reduce-scatter.22
  1702.9 146.5 reduce-scatter.20
  1852.9 117.5 reduce-scatter.10
  1974.1 147.0 reduce-scatter.16
